TPU v7x, 512 devices: a whole 4x8x8 slice. The times are simulated.
512 devices in a mesh: shards: 16 (over z, core), tensor: 4 (over x), sections: 8 (over y).
Axes of the slice: x: 4, y: 8, z: 8, core: 2. Of those that a mesh axis runs over, the one named last changes fastest.
Arguments:
- replica_grads: bfloat16 [16, 8, 2, 1536, 512], P('shards', 'sections', None, None, 'tensor'), may hold values from -6 to 6
- error_feedback: bfloat16 [16, 8, 2, 1536, 512], P('shards', 'sections', None, None, 'tensor'), may hold values from -3 to 3
- q_start: float32 [8, 2, 512, 32], P('sections', None, 'tensor'), may hold values from -0.25 to 0.25
- gram_root: float32 [8, 2, 32, 32], P('sections'), may hold values from -2 to 2
- momentum: float32 [8, 2, 1536, 512], P('sections', None, 'shards', 'tensor'), may hold values from -1.2 to 1.2
- weights: float32 [8, 2, 1536, 512], P('sections', None, 'shards', 'tensor'), may hold values from -3 to 3
- router_partials: bfloat16 [512, 1536, 40], P(('shards', 'tensor', 'sections')), may hold values from -12 to 12
- gain_partials: bfloat16 [512, 2, 1536], P(('shards', 'tensor', 'sections')), may hold values from -12 to 12
- router_momentum: float32 [1536, 40], P('shards'), may hold values from -1.2 to 1.2
- router_weights: float32 [1536, 40], P('shards'), may hold values from -3 to 3
- gain_momentum: float32 [2, 1536], P(None, 'shards'), may hold values from -1.2 to 1.2
- gain_weights: float32 [2, 1536], P(None, 'shards'), may hold values from 0.1 to 1.9
Outputs:
- new_error: bfloat16 [16, 8, 2, 1536, 512], P('shards', 'sections', None, None, 'tensor')
- new_momentum: float32 [8, 2, 1536, 512], P('sections', None, 'shards', 'tensor')
- new_weights: float32 [8, 2, 1536, 512], P('sections', None, None, 'tensor')
- new_router_momentum: float32 [1536, 40], P('shards')
- new_router_weights: float32 [1536, 40], replicated
- new_gain_momentum: float32 [2, 1536], P(None, 'shards')
- new_gain_weights: float32 [2, 1536], replicated
All inputs are finite; a program needn't handle non-finite values.
Results may differ from a plain program's by a relative error of at most 0.001.
Values sent between devices are 32-bit elements; how exact they have to be, the bound alone decides.
No kernel may reach another device: no remote copies, remote signals or barrier semaphores. Data moves between devices by JAX's collectives and lax.ppermute only.
A program may use at most 64 MiB of HBM per device.

v0:
```python
import jax
import jax.numpy as jnp
from jax import lax
from jax.sharding import PartitionSpec as P

momentum_decay = 0.9
step_size = 0.5
lanes = 128
rank = 32
highest = lax.Precision.HIGHEST
f32 = jnp.float32
plane = ("shards", "tensor")
sheet = ("tensor", "sections")


def exchange(blocks, axes):
    return lax.all_to_all(blocks, axes, 0, 0, tiled=True)


def spread(row, count, axes):
    return exchange(jnp.broadcast_to(row, (count,) + row.shape[1:]), axes)


def per_device(
    replica_grads,
    error_feedback,
    q_start,
    gram_root,
    momentum,
    weights,
    router_partials,
    gain_partials,
    router_momentum,
    router_weights,
    gain_momentum,
    gain_weights,
):
    shard_count = lax.axis_size("shards")
    tensor_count = lax.axis_size("tensor")
    section_count = lax.axis_size("sections")
    plane_count = shard_count * tensor_count
    sheet_count = tensor_count * section_count
    shard_index = lax.axis_index("shards")
    rows = momentum.shape[2]
    width = gain_partials.shape[2]
    start = shard_index * rows
    blocks = width // lanes
    base_rows = weights[0] - step_size * momentum_decay * momentum[0]
    base = lax.all_gather(base_rows, "shards", axis=1, tiled=True)
    columns = jnp.concatenate([router_partials[0].T, gain_partials[0]], 0).astype(f32)
    count = columns.shape[0]
    strips = columns.reshape(count, blocks, lanes).transpose(1, 0, 2).reshape(count * blocks, lanes)
    total_rows = plane_count * section_count
    strips = jnp.pad(strips, ((0, total_rows - count * blocks), (0, 0)))
    strips = strips.reshape(tensor_count, section_count, shard_count, lanes).transpose(1, 2, 0, 3)
    strips = strips.reshape(section_count, plane_count, lanes)
    strips = exchange(strips, "sections").sum(0)
    combined = replica_grads[0, 0].astype(f32) + error_feedback[0, 0].astype(f32)
    q_rows = q_start[0].transpose(0, 2, 1)
    p_rows = jnp.einsum("krf,kdf->krd", q_rows, combined, precision=highest)
    p_row = exchange(p_rows.reshape(plane_count, width), plane).sum(0, keepdims=True)
    packed = jnp.concatenate([jnp.broadcast_to(p_row, (plane_count, width)), strips], 1)
    packed = exchange(packed, plane)
    strip = packed[:, width:].sum(0, keepdims=True)
    p_avg = packed[:, :width].reshape(2, rank, width) / shard_count
    p_hat = jnp.einsum("krd,krt->ktd", p_avg, gram_root[0], precision=highest)
    q_local = jnp.einsum("ktd,kdf->ktf", p_hat, combined, precision=highest)
    small_base = jnp.concatenate(
        [
            router_weights.T - step_size * momentum_decay * router_momentum.T,
            gain_weights - step_size * momentum_decay * gain_momentum,
        ],
        0,
    )
    small_base = jnp.pad(small_base, ((0, 48 - count), (0, lanes - rows)))
    bundle = jnp.concatenate(
        [q_local.reshape(2 * rank, lanes), small_base, jnp.pad(strip, ((0, 7), (0, 0)))], 0
    )
    bundle = lax.all_gather(bundle, "shards", axis=0, tiled=False)
    q_avg = (bundle[:, : 2 * rank].sum(0) / shard_count).reshape(2, rank, lanes)
    strip_set = bundle[:, 2 * rank + 48]
    small_base = (
        bundle[:, 2 * rank : 2 * rank + count, :rows].transpose(1, 0, 2).reshape(count, width)
    )
    small = spread(strip_set[None], sheet_count, sheet)
    small = small.reshape(total_rows, lanes)[: count * blocks]
    small = (
        small.reshape(blocks, count, lanes).transpose(1, 0, 2).reshape(count, width) / shard_count
    )
    approx = jnp.einsum("ktd,ktf->kdf", p_hat, q_avg, precision=highest)
    new_error = (combined - approx).astype(jnp.bfloat16)[None, None]
    new_weights = (base - step_size * approx)[None]
    approx_rows = lax.dynamic_slice_in_dim(approx, start, rows, 1)
    new_momentum = momentum_decay * momentum + approx_rows[None]
    own = lax.dynamic_slice_in_dim(small, start, rows, 1)
    new_router_momentum = momentum_decay * router_momentum + own[:-2].T
    new_gain_momentum = momentum_decay * gain_momentum + own[-2:]
    new_small = small_base - step_size * small
    return (
        new_error,
        new_momentum,
        new_weights,
        new_router_momentum,
        new_small[:-2].T,
        new_gain_momentum,
        new_small[-2:],
    )


def solution(mesh):
    return jax.shard_map(
        per_device,
        mesh=mesh,
        in_specs=(
            P("shards", "sections", None, None, "tensor"),
            P("shards", "sections", None, None, "tensor"),
            P("sections", None, "tensor", None),
            P("sections", None, None, None),
            P("sections", None, "shards", "tensor"),
            P("sections", None, "shards", "tensor"),
            P(("shards", "tensor", "sections"), None, None),
            P(("shards", "tensor", "sections"), None, None),
            P("shards", None),
            P("shards", None),
            P(None, "shards"),
            P(None, "shards"),
        ),
        out_specs=(
            P("shards", "sections", None, None, "tensor"),
            P("sections", None, "shards", "tensor"),
            P("sections", None, None, "tensor"),
            P("shards", None),
            P(),
            P(None, "shards"),
            P(),
        ),
        check_vma=False,
    )
```

profile of v0, /device:TPU:1, one launch (start us, length us, event | category | flops | bytes accessed | tf_op | source)
XLA Modules:
  0.0 150.9 jit_solution(3413235072184591693)
XLA Ops:
  7.2 0.8 concatenate.18
  8.0 1.0 concatenate.17
  9.2 0.8 copy.30
  10.0 7.7 %all-to-all-start.1 = ((f32[8,64,128]{2,1,0:T(8,128)}), f32[8,64,128]{2,1,0:T(8,128)S(1)}, u32[]{:S(2)}, u32[]{:S(2)}) async-start(f32[8,64,128]{2,1,0:T(8,128)} %copy.30), calls=%async_computation.1 | async-start | bytes 524288 | tf_op jit(solution)/shard_map/all_to_all | solution.py:17
  17.6 1.8 %fusion.3 = f32[2,1536,32]{1,2,0:T(8,128)S(1)} fusion(bf16[1,1,2,1536,128]{4,3,2,1,0:T(8,128)(2,1)S(1)} %copy-done.1, bf16[1,1,2,1536,128]{4,3,2,1,0:T(8,128)(2,1)S(1)} %copy-done.2, f32[1,2,128,32]{2,3,1,0:T(8,128)S(1)} %copy-done), kind=kOutput, calls=%fused_computation.5 | convolution fusion | flops 152174592 | bytes 1998848 | tf_op jit(solution)/shard_map/krf,kdf->krd/dot_general | solution.py:60
  19.5 1.2 copy.27
  20.6 6.4 %all-to-all-done.1 = f32[8,64,128]{2,1,0:T(8,128)S(1)} async-done(((f32[8,64,128]{2,1,0:T(8,128)}), f32[8,64,128]{2,1,0:T(8,128)S(1)}, u32[]{:S(2)}, u32[]{:S(2)}) %all-to-all-start.1) | async-done | bytes 262176 | tf_op jit(solution)/shard_map/all_to_all | solution.py:17
  27.0 16.8 %all-to-all-start = ((f32[64,1,1536]{2,1,0:T(1,128)}), f32[64,1,1536]{2,1,0:T(1,128)S(1)}, u32[]{:S(2)}, u32[]{:S(2)}) async-start(f32[64,1,1536]{2,1,0:T(1,128)} %copy.27), calls=%async_computation | async-start | bytes 786432 | tf_op jit(solution)/shard_map/all_to_all | solution.py:17
  43.9 14.6 %all-to-all-done = f32[64,1,1536]{2,1,0:T(1,128)S(1)} async-done(((f32[64,1,1536]{2,1,0:T(1,128)}), f32[64,1,1536]{2,1,0:T(1,128)S(1)}, u32[]{:S(2)}, u32[]{:S(2)}) %all-to-all-start) | async-done | bytes 393248 | tf_op jit(solution)/shard_map/all_to_all | solution.py:17
  58.7 1.1 all_to_all.23
  59.8 6.0 %all-to-all-start.2 = ((f32[64,1,1664]{2,1,0:T(1,128)}), f32[64,1,1664]{2,1,0:T(1,128)S(1)}, u32[]{:S(2)}, u32[]{:S(2)}) async-start(f32[64,1,1664]{2,1,0:T(1,128)} %all_to_all.23), calls=%async_computation.2 | async-start | bytes 851968 | tf_op jit(solution)/shard_map/all_to_all | solution.py:17
  65.9 15.3 %all-to-all-done.2 = f32[64,1,1664]{2,1,0:T(1,128)S(1)} async-done(((f32[64,1,1664]{2,1,0:T(1,128)}), f32[64,1,1664]{2,1,0:T(1,128)S(1)}, u32[]{:S(2)}, u32[]{:S(2)}) %all-to-all-start.2) | async-done | bytes 426016 | tf_op jit(solution)/shard_map/all_to_all | solution.py:17
  81.8 1.1 fusion.1
  82.9 19.7 %all-gather = f32[1920,128]{1,0:T(8,128)S(1)} all-gather(f32[120,128]{1,0:T(8,128)S(1)} %select_maximum_fusion), channel_id=2, replica_groups=mesh['shards'=16,'tensor'=4,'sections'=8] {'shards'}, dimensions={0}, use_global_device_ids=true | all-gather | bytes 1044480 | tf_op jit(solution)/shard_map/all_gather | solution.py:79
  102.6 0.9 copy-done.3
  103.5 2.6 %fusion.11 = f32[2,1536,128]{2,1,0:T(8,128)S(1)} fusion(f32[2,1536,32]{1,2,0:T(8,128)S(1)} %fusion.7, f32[2,32,128]{2,1,0:T(8,128)S(1)} %bitcast.89), kind=kOutput, calls=%fused_computation.36 | convolution fusion | flops 150994944 | bytes 1998848 | tf_op jit(solution)/shard_map/ktd,ktf->kdf/dot_general | solution.py:90
  106.1 0.7 multiply_subtract_fusion
  106.8 0.8 slice.43
  107.7 0.7 broadcast_in_dim.31
  108.4 4.6 %all-to-all-start.3 = ((f32[32,16,128]{2,1,0:T(8,128)}), f32[32,16,128]{2,1,0:T(8,128)}, u32[]{:S(2)}, u32[]{:S(2)}) async-start(f32[32,16,128]{2,1,0:T(8,128)} %broadcast_in_dim.31), calls=%async_computation.3 | async-start | bytes 524288 | tf_op jit(solution)/shard_map/all_to_all | solution.py:17
  113.0 1.0 slice.45
  114.2 0.9 reshape.78
  115.1 8.4 %all-to-all-done.3 = f32[32,16,128]{2,1,0:T(8,128)} async-done(((f32[32,16,128]{2,1,0:T(8,128)}), f32[32,16,128]{2,1,0:T(8,128)}, u32[]{:S(2)}, u32[]{:S(2)}) %all-to-all-start.3) | async-done | bytes 262176 | tf_op jit(solution)/shard_map/all_to_all | solution.py:17
  123.5 1.8 %slice_multiply_fusion.1 = (f32[504,128]{1,0:T(8,128)}, f32[504,128]{1,0:T(8,128)}) fusion(f32[512,128]{1,0:T(8,128)} %bitcast.22), kind=kLoop, calls=%fused_computation.16 | loop fusion | flops 129024 | bytes 774144 | tf_op jit(solution)/shard_map/mul | solution.py:98
  125.3 1.7 %mul.77 = f32[12,42,128]{2,1,0:T(8,128)} reshape(f32[504,128]{1,0:T(8,128)} %get-tuple-element.9) | data formatting | bytes 516096 | tf_op jit(solution)/shard_map/mul | solution.py:98
  127.0 1.1 copy.34
  128.3 0.6 slice.47
  129.0 1.0 div.36
  130.8 0.7 fusion.10
  131.5 0.7 slice_bitcast_fusion
  132.2 8.7 %all-gather.4.cloned.1.call-done = f32[1,2,1536,128]{3,2,1,0:T(8,128)} async-done(((f32[1,2,96,128]{3,2,1,0:T(8,128)}), f32[1,2,1536,128]{3,2,1,0:T(8,128)}) %all-gather.4.cloned.1.call-update) | async-done | bytes 1572880 | tf_op jit(solution)/shard_map/all_gather | solution.py:49
  140.9 3.2 %fusion = (f32[1,2,1536,128]{3,2,1,0:T(8,128)}, bf16[1,1,2,1536,128]{4,3,2,1,0:T(8,128)(2,1)}) fusion(f32[1,2,1536,128]{3,2,1,0:T(8,128)} %all-gather.4.cloned.1.call-done, f32[2,1536,128]{2,1,0:T(8,128)S(1)} %fusion.11, bf16[1,1,2,1536,128]{4,3,2,1,0:T(8,128)(2,1)S(1)} %copy-done.1, bf16[1,1,2,1536,128]{4,3,2,1,0:T(8,128)(2,1)S(1)} %copy-done.2), kind=kLoop, calls=%fused_computation.1 | loop fusion | flops 2752512 | bytes 7077888 | tf_op jit(solution)/shard_map/broadcast_in_dim | solution.py:92
  (56 shorter events, 2.5 us)
Async XLA Ops:
  7.2 10.5 %copy-start = (f32[1,2,128,32]{2,3,1,0:T(8,128)S(1)}, f32[1,2,128,32]{2,3,1,0:T(8,128)}, u32[]{:S(2)}) copy-start(f32[1,2,128,32]{2,3,1,0:T(8,128)} %param.14) | copy-start | bytes 98308
  7.2 10.4 %copy-start.1 = (bf16[1,1,2,1536,128]{4,3,2,1,0:T(8,128)(2,1)S(1)}, bf16[1,1,2,1536,128]{4,3,2,1,0:T(8,128)(2,1)}, u32[]{:S(2)}) copy-start(bf16[1,1,2,1536,128]{4,3,2,1,0:T(8,128)(2,1)} %param.13) | copy-start | bytes 2359300
  7.2 10.4 %copy-start.2 = (bf16[1,1,2,1536,128]{4,3,2,1,0:T(8,128)(2,1)S(1)}, bf16[1,1,2,1536,128]{4,3,2,1,0:T(8,128)(2,1)}, u32[]{:S(2)}) copy-start(bf16[1,1,2,1536,128]{4,3,2,1,0:T(8,128)(2,1)} %param.12) | copy-start | bytes 2359300
  10.0 17.1 %all-to-all-start.1 = ((f32[8,64,128]{2,1,0:T(8,128)}), f32[8,64,128]{2,1,0:T(8,128)S(1)}, u32[]{:S(2)}, u32[]{:S(2)}) async-start(f32[8,64,128]{2,1,0:T(8,128)} %copy.30), calls=%async_computation.1 | async-start | bytes 524288 | tf_op jit(solution)/shard_map/all_to_all | solution.py:17
  27.0 31.4 %all-to-all-start = ((f32[64,1,1536]{2,1,0:T(1,128)}), f32[64,1,1536]{2,1,0:T(1,128)S(1)}, u32[]{:S(2)}, u32[]{:S(2)}) async-start(f32[64,1,1536]{2,1,0:T(1,128)} %copy.27), calls=%async_computation | async-start | bytes 786432 | tf_op jit(solution)/shard_map/all_to_all | solution.py:17
  43.8 22.0 %copy-start.12 = (f32[2,96]{1,0:T(2,128)S(1)}, f32[2,96]{1,0:T(2,128)}, u32[]{:S(2)}) copy-start(f32[2,96]{1,0:T(2,128)} %param.22) | copy-start | bytes 2308
  43.8 22.0 %copy-start.13 = (f32[2,96]{1,0:T(2,128)S(1)}, f32[2,96]{1,0:T(2,128)}, u32[]{:S(2)}) copy-start(f32[2,96]{1,0:T(2,128)} %param.23) | copy-start | bytes 2308
  43.8 22.0 %copy-start.9 = (f32[96,40]{0,1:T(8,128)S(1)}, f32[96,40]{0,1:T(8,128)}, u32[]{:S(2)}) copy-start(f32[96,40]{0,1:T(8,128)} %param.20) | copy-start | bytes 46084
  43.8 22.0 %copy-start.11 = (f32[96,40]{0,1:T(8,128)S(1)}, f32[96,40]{0,1:T(8,128)}, u32[]{:S(2)}) copy-start(f32[96,40]{0,1:T(8,128)} %param.21) | copy-start | bytes 46084
  58.7 22.5 %copy-start.10 = (f32[1,2,32,32]{3,2,1,0:T(8,128)S(1)}, f32[1,2,32,32]{3,2,1,0:T(8,128)}, u32[]{:S(2)}) copy-start(f32[1,2,32,32]{3,2,1,0:T(8,128)} %param.15) | copy-start | bytes 24580
  59.8 21.4 %all-to-all-start.2 = ((f32[64,1,1664]{2,1,0:T(1,128)}), f32[64,1,1664]{2,1,0:T(1,128)S(1)}, u32[]{:S(2)}, u32[]{:S(2)}) async-start(f32[64,1,1664]{2,1,0:T(1,128)} %all_to_all.23), calls=%async_computation.2 | async-start | bytes 851968 | tf_op jit(solution)/shard_map/all_to_all | solution.py:17
  65.8 75.2 %all-gather.4.cloned.1.call-start = ((), (), s32[]{:S(2)}) async-start(), calls=%async_computation.4 | async-start | bytes 1671168 | tf_op jit(solution)/shard_map/all_gather | solution.py:49
  102.5 0.9 copy-start.3
  102.5 3.6 %copy-start.7 = (f32[1,2,96,128]{3,2,1,0:T(8,128)S(1)}, f32[1,2,96,128]{3,2,1,0:T(8,128)}, u32[]{:S(2)}) copy-start(f32[1,2,96,128]{3,2,1,0:T(8,128)} %param.17) | copy-start | bytes 294916
  102.5 3.6 %copy-start.8 = (f32[1,2,96,128]{3,2,1,0:T(8,128)S(1)}, f32[1,2,96,128]{3,2,1,0:T(8,128)}, u32[]{:S(2)}) copy-start(f32[1,2,96,128]{3,2,1,0:T(8,128)} %param.16) | copy-start | bytes 294916
  108.4 15.1 %all-to-all-start.3 = ((f32[32,16,128]{2,1,0:T(8,128)}), f32[32,16,128]{2,1,0:T(8,128)}, u32[]{:S(2)}, u32[]{:S(2)}) async-start(f32[32,16,128]{2,1,0:T(8,128)} %broadcast_in_dim.31), calls=%async_computation.3 | async-start | bytes 524288 | tf_op jit(solution)/shard_map/all_to_all | solution.py:17
  123.5 4.7 %copy-start.4 = (f32[42,1536]{1,0:T(8,128)S(1)}, f32[42,1536]{1,0:T(8,128)}, u32[]{:S(2)}) copy-start(f32[42,1536]{1,0:T(8,128)} %reshape.78) | copy-start | bytes 774148
  128.2 0.7 copy-start.5
  129.9 1.6 %copy-start.6 = (f32[42,1536]{1,0:T(8,128)S(1)}, f32[42,1536]{1,0:T(8,128)}, u32[]{:S(2)}) copy-start(f32[42,1536]{1,0:T(8,128)} %copy-done.5) | copy-start | bytes 774148
Sparse Core Ops, SparseCore 0:
  107.0 33.9 all-gather.3
where the time goes:
time: 152 us; the launch traced here: 151 us
  waiting for transfers between devices  53.4 us (35%)
  starting transfers between devices  35 us (23%)
  blocking collectives  19.7 us (13%)
  local copies, waits for them, and re-layouts  14.9 us (10%)
  between operations  14.4 us (9%)
  other arithmetic  7.52 us (5%)
  matrix products  6.02 us (4%)
    all_to_all x4, waiting for transfers between devices, exchange(): return lax.all_to_all(blocks, axes, 0, 0, tiled=True)  44.6 us
    all_to_all x4, starting transfers between devices, exchange(): return lax.all_to_all(blocks, axes, 0, 0, tiled=True)  35 us
    all_gather x1, blocking collectives, per_device(): bundle = lax.all_gather(bundle, 'shards', axis=0, tiled=False)  19.7 us
    all_gather x1, waiting for transfers between devices, per_device(): base = lax.all_gather(base_rows, 'shards', axis=1, tiled=True)  8.7 us
    broadcast_in_dim x1, other arithmetic, per_device(): new_weights = (base - step_size * approx)[None]  3.16 us
  transfers between devices with their start and end apart: 5, of which 5 were waited for; matrix products, arithmetic and copies ran while one was open for 10% of the time, Pallas kernels for 0%

commit v1 on v0

--- a/solution.py
+++ b/solution.py
@@ -46,7 +46,9 @@
     start = shard_index * rows
     blocks = width // lanes
     base_rows = weights[0] - step_size * momentum_decay * momentum[0]
-    base = lax.all_gather(base_rows, "shards", axis=1, tiled=True)
+    base = jnp.concatenate(
+        lax.all_to_all(jnp.stack([base_rows] * lax.axis_size("shards")), "shards", 0, 0), axis=1
+    )
     columns = jnp.concatenate([router_partials[0].T, gain_partials[0]], 0).astype(f32)
     count = columns.shape[0]
     strips = columns.reshape(count, blocks, lanes).transpose(1, 0, 2).reshape(count * blocks, lanes)

time: 152 us -> 162 us (1.066)
  waiting for transfers between devices: 53.4 us -> 69.3 us
  between operations: 14.4 us -> 1.03 us
  starting transfers between devices: 35 us -> 40.4 us
  local copies, waits for them, and re-layouts: 14.9 us -> 17 us
    all_to_all x0 -> x1, waiting for transfers between devices: none -> 27.8 us  [per_device(): lax.all_to_all(jnp.stack([base_rows] * lax.axis_size('shards')), 'shards'...]
    all_gather x1 -> x0, waiting for transfers between devices: 8.7 us -> none  [per_device(): base = lax.all_gather(base_rows, 'shards', axis=1, tiled=True)]
    all_to_all x0 -> x1, starting transfers between devices: none -> 6.13 us  [per_device(): lax.all_to_all(jnp.stack([base_rows] * lax.axis_size('shards')), 'shards'...]
    broadcast_in_dim x1 -> x0, other arithmetic: 3.16 us -> none  [per_device(): new_weights = (base - step_size * approx)[None]]
    all_to_all x4, waiting for transfers between devices: 44.6 us -> 41.5 us  [exchange(): return lax.all_to_all(blocks, axes, 0, 0, tiled=True)]
  transfers between devices with their start and end apart: 5 -> 5, of which waited for: 5 -> 5; matrix products, arithmetic and copies ran while one was open for 10% -> 12% of each run, Pallas kernels for 0% -> 0%
where the time goes in v1:
time: 162 us; the launch traced here: 161 us
  waiting for transfers between devices  69.3 us (43%)
  starting transfers between devices  40.4 us (25%)
  blocking collectives  19.7 us (12%)
  local copies, waits for them, and re-layouts  17 us (10%)
  other arithmetic  7.11 us (4%)
  matrix products  7.02 us (4%)
    all_to_all x4, waiting for transfers between devices, exchange(): return lax.all_to_all(blocks, axes, 0, 0, tiled=True)  41.5 us
    all_to_all x4, starting transfers between devices, exchange(): return lax.all_to_all(blocks, axes, 0, 0, tiled=True)  34.2 us
    all_to_all x1, waiting for transfers between devices, per_device(): lax.all_to_all(jnp.stack([base_rows] * lax.axis_size('shards')), 'shards'...  27.8 us
    all_gather x1, blocking collectives, per_device(): bundle = lax.all_gather(bundle, 'shards', axis=0, tiled=False)  19.7 us
    all_to_all x1, starting transfers between devices, per_device(): lax.all_to_all(jnp.stack([base_rows] * lax.axis_size('shards')), 'shards'...  6.13 us
    dot_general x1, matrix products, per_device(): approx = jnp.einsum('ktd,ktf->kdf', p_hat, q_avg, precision=highest)  3.62 us
  transfers between devices with their start and end apart: 5, of which 5 were waited for; matrix products, arithmetic and copies ran while one was open for 12% of the time, Pallas kernels for 0%

profile of v1, /device:TPU:1, one launch (start us, length us, event | category | flops | bytes accessed | tf_op | source)
XLA Modules:
  0.0 161.5 jit_solution(18408578012392421334)
XLA Ops:
  0.7 0.8 concatenate.18
  1.5 1.0 concatenate.17
  2.7 0.8 copy.30
  3.4 7.7 %all-to-all-start.1 = ((f32[8,64,128]{2,1,0:T(8,128)}), f32[8,64,128]{2,1,0:T(8,128)S(1)}, u32[]{:S(2)}, u32[]{:S(2)}) async-start(f32[8,64,128]{2,1,0:T(8,128)} %copy.30), calls=%async_computation.1 | async-start | bytes 524288 | tf_op jit(solution)/shard_map/all_to_all | solution.py:17
  11.1 1.8 %fusion.2 = f32[2,1536,32]{1,2,0:T(8,128)S(1)} fusion(bf16[1,1,2,1536,128]{4,3,2,1,0:T(8,128)(2,1)S(1)} %copy-done.1, bf16[1,1,2,1536,128]{4,3,2,1,0:T(8,128)(2,1)S(1)} %copy-done.2, f32[1,2,128,32]{2,3,1,0:T(8,128)S(1)} %copy-done), kind=kOutput, calls=%fused_computation.4 | convolution fusion | flops 152174592 | bytes 1998848 | tf_op jit(solution)/shard_map/krf,kdf->krd/dot_general | solution.py:62
  12.9 1.2 copy.27
  14.1 6.4 %all-to-all-done.1 = f32[8,64,128]{2,1,0:T(8,128)S(1)} async-done(((f32[8,64,128]{2,1,0:T(8,128)}), f32[8,64,128]{2,1,0:T(8,128)S(1)}, u32[]{:S(2)}, u32[]{:S(2)}) %all-to-all-start.1) | async-done | bytes 262176 | tf_op jit(solution)/shard_map/all_to_all | solution.py:17
  20.5 16.8 %all-to-all-start = ((f32[64,1,1536]{2,1,0:T(1,128)}), f32[64,1,1536]{2,1,0:T(1,128)S(1)}, u32[]{:S(2)}, u32[]{:S(2)}) async-start(f32[64,1,1536]{2,1,0:T(1,128)} %copy.27), calls=%async_computation | async-start | bytes 786432 | tf_op jit(solution)/shard_map/all_to_all | solution.py:17
  37.3 14.6 %all-to-all-done = f32[64,1,1536]{2,1,0:T(1,128)S(1)} async-done(((f32[64,1,1536]{2,1,0:T(1,128)}), f32[64,1,1536]{2,1,0:T(1,128)S(1)}, u32[]{:S(2)}, u32[]{:S(2)}) %all-to-all-start) | async-done | bytes 393248 | tf_op jit(solution)/shard_map/all_to_all | solution.py:17
  52.2 1.1 all_to_all.26
  53.2 6.0 %all-to-all-start.2 = ((f32[64,1,1664]{2,1,0:T(1,128)}), f32[64,1,1664]{2,1,0:T(1,128)S(1)}, u32[]{:S(2)}, u32[]{:S(2)}) async-start(f32[64,1,1664]{2,1,0:T(1,128)} %all_to_all.26), calls=%async_computation.2 | async-start | bytes 851968 | tf_op jit(solution)/shard_map/all_to_all | solution.py:17
  59.3 15.3 %all-to-all-done.2 = f32[64,1,1664]{2,1,0:T(1,128)S(1)} async-done(((f32[64,1,1664]{2,1,0:T(1,128)}), f32[64,1,1664]{2,1,0:T(1,128)S(1)}, u32[]{:S(2)}, u32[]{:S(2)}) %all-to-all-start.2) | async-done | bytes 426016 | tf_op jit(solution)/shard_map/all_to_all | solution.py:17
  75.2 1.1 fusion
  76.3 19.7 %all-gather = f32[1920,128]{1,0:T(8,128)S(1)} all-gather(f32[120,128]{1,0:T(8,128)S(1)} %select_maximum_fusion), channel_id=2, replica_groups=mesh['shards'=16,'tensor'=4,'sections'=8] {'shards'}, dimensions={0}, use_global_device_ids=true | all-gather | bytes 1044480 | tf_op jit(solution)/shard_map/all_gather | solution.py:81
  96.0 1.0 copy-done.3
  97.0 0.7 broadcast_in_dim.31
  97.7 3.9 %all-to-all-start.4 = ((f32[32,16,128]{2,1,0:T(8,128)}), f32[32,16,128]{2,1,0:T(8,128)S(1)}, u32[]{:S(2)}, u32[]{:S(2)}) async-start(f32[32,16,128]{2,1,0:T(8,128)} %broadcast_in_dim.31), calls=%async_computation.4 | async-start | bytes 524288 | tf_op jit(solution)/shard_map/all_to_all | solution.py:17
  101.6 3.6 %fusion.10 = f32[2,1536,128]{2,1,0:T(8,128)S(1)} fusion(f32[2,1536,32]{1,2,0:T(8,128)} %copy-done.4, f32[2,32,128]{2,1,0:T(8,128)S(1)} %bitcast.91), kind=kOutput, calls=%fused_computation.35 | convolution fusion | flops 150994944 | bytes 1998848 | tf_op jit(solution)/shard_map/ktd,ktf->kdf/dot_general | solution.py:92
  105.2 1.6 subtract_bitcast_fusion
  106.8 5.2 %all-to-all-done.4 = f32[32,16,128]{2,1,0:T(8,128)S(1)} async-done(((f32[32,16,128]{2,1,0:T(8,128)}), f32[32,16,128]{2,1,0:T(8,128)S(1)}, u32[]{:S(2)}, u32[]{:S(2)}) %all-to-all-start.4) | async-done | bytes 262176 | tf_op jit(solution)/shard_map/all_to_all | solution.py:17
  112.1 1.3 stack.5
  113.4 6.1 %all-to-all-start.3 = ((f32[16,2,96,128]{3,2,1,0:T(8,128)}), f32[16,2,96,128]{3,2,1,0:T(8,128)}, u32[]{:S(2)}, u32[]{:S(2)}) async-start(f32[16,2,96,128]{3,2,1,0:T(8,128)} %stack.5), calls=%async_computation.3 | async-start | bytes 3145728 | tf_op jit(solution)/shard_map/all_to_all | solution.py:50
  119.5 1.0 slice.45
  120.7 0.9 reshape.84
  121.6 1.8 %slice_multiply_fusion.1 = (f32[504,128]{1,0:T(8,128)}, f32[504,128]{1,0:T(8,128)}) fusion(f32[512,128]{1,0:T(8,128)} %bitcast.87), kind=kLoop, calls=%fused_computation.15 | loop fusion | flops 129024 | bytes 774144 | tf_op jit(solution)/shard_map/mul | solution.py:100
  123.4 1.7 %mul.77 = f32[12,42,128]{2,1,0:T(8,128)} reshape(f32[504,128]{1,0:T(8,128)} %get-tuple-element.9) | data formatting | bytes 516096 | tf_op jit(solution)/shard_map/mul | solution.py:100
  125.1 1.1 copy.35
  127.1 1.0 div.36
  129.6 0.7 slice_bitcast_fusion
  130.3 27.8 %all-to-all-done.3 = f32[16,2,96,128]{3,2,1,0:T(8,128)} async-done(((f32[16,2,96,128]{3,2,1,0:T(8,128)}), f32[16,2,96,128]{3,2,1,0:T(8,128)}, u32[]{:S(2)}, u32[]{:S(2)}) %all-to-all-start.3) | async-done | bytes 1572896 | tf_op jit(solution)/shard_map/all_to_all | solution.py:50
  158.1 1.5 copy.32
  159.7 1.8 %bitcast_subtract_fusion = (f32[2,1536,128]{2,1,0:T(8,128)}, bf16[1,1,2,1536,128]{4,3,2,1,0:T(8,128)(2,1)}) fusion(f32[2,16,96,128]{3,2,1,0:T(8,128)S(1)} %copy.32, f32[2,1536,128]{2,1,0:T(8,128)S(1)} %fusion.10, bf16[1,1,2,1536,128]{4,3,2,1,0:T(8,128)(2,1)S(1)} %copy-done.1, bf16[1,1,2,1536,128]{4,3,2,1,0:T(8,128)(2,1)S(1)} %copy-done.2), kind=kLoop, calls=%fused_computation | loop fusion | flops 2752512 | bytes 7077888 | tf_op jit(solution)/shard_map/sub | solution.py:94
  (59 shorter events, 3.7 us)
Async XLA Ops:
  0.6 10.5 %copy-start = (f32[1,2,128,32]{2,3,1,0:T(8,128)S(1)}, f32[1,2,128,32]{2,3,1,0:T(8,128)}, u32[]{:S(2)}) copy-start(f32[1,2,128,32]{2,3,1,0:T(8,128)} %param.14) | copy-start | bytes 98308
  0.6 10.4 %copy-start.1 = (bf16[1,1,2,1536,128]{4,3,2,1,0:T(8,128)(2,1)S(1)}, bf16[1,1,2,1536,128]{4,3,2,1,0:T(8,128)(2,1)}, u32[]{:S(2)}) copy-start(bf16[1,1,2,1536,128]{4,3,2,1,0:T(8,128)(2,1)} %param.13) | copy-start | bytes 2359300
  0.7 10.4 %copy-start.2 = (bf16[1,1,2,1536,128]{4,3,2,1,0:T(8,128)(2,1)S(1)}, bf16[1,1,2,1536,128]{4,3,2,1,0:T(8,128)(2,1)}, u32[]{:S(2)}) copy-start(bf16[1,1,2,1536,128]{4,3,2,1,0:T(8,128)(2,1)} %param.12) | copy-start | bytes 2359300
  3.4 17.1 %all-to-all-start.1 = ((f32[8,64,128]{2,1,0:T(8,128)}), f32[8,64,128]{2,1,0:T(8,128)S(1)}, u32[]{:S(2)}, u32[]{:S(2)}) async-start(f32[8,64,128]{2,1,0:T(8,128)} %copy.30), calls=%async_computation.1 | async-start | bytes 524288 | tf_op jit(solution)/shard_map/all_to_all | solution.py:17
  20.5 31.4 %all-to-all-start = ((f32[64,1,1536]{2,1,0:T(1,128)}), f32[64,1,1536]{2,1,0:T(1,128)S(1)}, u32[]{:S(2)}, u32[]{:S(2)}) async-start(f32[64,1,1536]{2,1,0:T(1,128)} %copy.27), calls=%async_computation | async-start | bytes 786432 | tf_op jit(solution)/shard_map/all_to_all | solution.py:17
  37.3 22.0 %copy-start.13 = (f32[2,96]{1,0:T(2,128)S(1)}, f32[2,96]{1,0:T(2,128)}, u32[]{:S(2)}) copy-start(f32[2,96]{1,0:T(2,128)} %param.22) | copy-start | bytes 2308
  37.3 22.0 %copy-start.14 = (f32[2,96]{1,0:T(2,128)S(1)}, f32[2,96]{1,0:T(2,128)}, u32[]{:S(2)}) copy-start(f32[2,96]{1,0:T(2,128)} %param.23) | copy-start | bytes 2308
  37.3 22.0 %copy-start.9 = (f32[96,40]{0,1:T(8,128)S(1)}, f32[96,40]{0,1:T(8,128)}, u32[]{:S(2)}) copy-start(f32[96,40]{0,1:T(8,128)} %param.20) | copy-start | bytes 46084
  37.3 22.0 %copy-start.12 = (f32[96,40]{0,1:T(8,128)S(1)}, f32[96,40]{0,1:T(8,128)}, u32[]{:S(2)}) copy-start(f32[96,40]{0,1:T(8,128)} %param.21) | copy-start | bytes 46084
  52.2 22.5 %copy-start.11 = (f32[1,2,32,32]{3,2,1,0:T(8,128)S(1)}, f32[1,2,32,32]{3,2,1,0:T(8,128)}, u32[]{:S(2)}) copy-start(f32[1,2,32,32]{3,2,1,0:T(8,128)} %param.15) | copy-start | bytes 24580
  53.2 21.4 %all-to-all-start.2 = ((f32[64,1,1664]{2,1,0:T(1,128)}), f32[64,1,1664]{2,1,0:T(1,128)S(1)}, u32[]{:S(2)}, u32[]{:S(2)}) async-start(f32[64,1,1664]{2,1,0:T(1,128)} %all_to_all.26), calls=%async_computation.2 | async-start | bytes 851968 | tf_op jit(solution)/shard_map/all_to_all | solution.py:17
  75.2 20.8 %copy-start.4 = (f32[2,1536,32]{1,2,0:T(8,128)}, f32[2,1536,32]{1,2,0:T(8,128)S(1)}, u32[]{:S(2)}) copy-start(f32[2,1536,32]{1,2,0:T(8,128)S(1)} %fusion.6) | copy-start | bytes 1179652
  96.0 1.0 copy-start.3
  97.7 14.4 %all-to-all-start.4 = ((f32[32,16,128]{2,1,0:T(8,128)}), f32[32,16,128]{2,1,0:T(8,128)S(1)}, u32[]{:S(2)}, u32[]{:S(2)}) async-start(f32[32,16,128]{2,1,0:T(8,128)} %broadcast_in_dim.31), calls=%async_computation.4 | async-start | bytes 524288 | tf_op jit(solution)/shard_map/all_to_all | solution.py:17
  112.1 1.3 copy-start.8
  113.4 44.7 %all-to-all-start.3 = ((f32[16,2,96,128]{3,2,1,0:T(8,128)}), f32[16,2,96,128]{3,2,1,0:T(8,128)}, u32[]{:S(2)}, u32[]{:S(2)}) async-start(f32[16,2,96,128]{3,2,1,0:T(8,128)} %stack.5), calls=%async_computation.3 | async-start | bytes 3145728 | tf_op jit(solution)/shard_map/all_to_all | solution.py:50
  121.6 4.7 %copy-start.5 = (f32[42,1536]{1,0:T(8,128)S(1)}, f32[42,1536]{1,0:T(8,128)}, u32[]{:S(2)}) copy-start(f32[42,1536]{1,0:T(8,128)} %reshape.84) | copy-start | bytes 774148
  126.3 2.6 %copy-start.10 = (f32[96,40]{0,1:T(8,128)S(1)}, f32[96,40]{0,1:T(8,128)}, u32[]{:S(2)}) copy-start(f32[96,40]{0,1:T(8,128)} %param.20) | copy-start | bytes 46084
  126.4 0.7 copy-start.6
  128.0 1.6 copy-start.7
